TPU v7x, 32 devices: a whole 2x2x4 slice. The times are simulated.
32 devices in a mesh: tbl: 16 (over z, x, core), hst: 2 (over y).
Axes of the slice: x: 2, y: 2, z: 4, core: 2. Of those that a mesh axis runs over, the one named last changes fastest.
Arguments:
- pooled: bfloat16 [8192, 512], P('tbl'), may hold values from -6 to 6
- w_up: bfloat16 [512, 4096], P(None, 'hst'), may hold values from -0.25 to 0.25
- grad_out: bfloat16 [8192, 4096], P('tbl', 'hst'), may hold values from -6 to 6
- owners: int32 [4, 8192, 8], P('hst', 'tbl'), may hold values from 0 to 15, all different within a row; in each aligned block of 512 rows (0 to 511, 512 to 1023, ..., all dimensions but the last counted through in order) at most 512 rows name the same one
- rows: int32 [4, 8192, 8], P('hst', 'tbl'), may hold values from 0 to 1023
- lookup_weight: bfloat16 [4, 8192, 8], P('hst', 'tbl'), may hold values from 0.25 to 2
- lens: int32 [4, 8192], P('hst', 'tbl'), may hold values from 4 to 8
- slot_map: int32 [16, 2, 2048], P('tbl', 'hst'), may hold values from 0 to 2047, each once within a row
- cache_weight: float32 [16, 2, 2048, 128], P('tbl', 'hst'), may hold values from -6 to 6
- cache_accum: float32 [16, 2, 2048], P('tbl', 'hst'), may hold values from 0.1 to 10
- evict_slots: int32 [16, 2, 256], P('tbl', 'hst'), may hold values from 0 to 2047, as said below
- evict_dest: int32 [16, 2, 256], P('tbl', 'hst'), may hold values from 0 to 1, as said below
- evict_count: int32 [16, 2], P('tbl', 'hst'), may hold values from 128 to 256
Outputs:
- grad_up: float32 [512, 4096], P('tbl', 'hst')
- new_weight: float32 [16, 2, 2048, 128], P('tbl', 'hst')
- new_accum: float32 [16, 2, 2048], P('tbl', 'hst')
- held_rows: float32 [16, 2, 2, 128, 128], P('tbl', 'hst')
- held_accum: float32 [16, 2, 2, 128], P('tbl', 'hst')
Inputs may be any that keep to these rules, and one draw needn't show every extreme that they name: The 8 owners of one bag differ. Among the 512 samples of one index of tbl and one table, no owner is named by more than 512 lookup positions, used or not; some owner is named by exactly 512 in some such block. `evict_slots`: the 256 slots of one device's list differ. `evict_dest`: among the used entries of one device, no holder appears more than 128 times, and one holder appears exactly 128 times.
All inputs are finite; a program needn't handle non-finite values.
Results may differ from a plain program's by a relative error of at most 0.0029.
Values may be sent and summed in bfloat16 or wider, within the bound.
A program may use at most 64 MiB of HBM per device.

v0:
```python
import jax
import jax.numpy as jnp
from jax import lax
from jax.sharding import PartitionSpec as P

LEARN_RATE = 0.05
EPSILON = 1e-08


def on_device(
    pooled,
    w_up,
    grad_out,
    owners,
    rows,
    lookup_weight,
    lens,
    slot_map,
    cache_weight,
    cache_accum,
    evict_slots,
    evict_dest,
    evict_count,
):
    tables_dev, batch_rows, bag_len = owners.shape
    slot_count = slot_map.shape[-1]
    rows_dev = slot_count // tables_dev
    emb_width = cache_weight.shape[-1]
    preact = jnp.dot(pooled, w_up, preferred_element_type=jnp.float32)
    sigmoid_z = jax.nn.sigmoid(preact)
    delta = (grad_out.astype(jnp.float32) * sigmoid_z * (1.0 + preact * (1.0 - sigmoid_z))).astype(
        jnp.bfloat16
    )
    feature_part = lax.dot_general(
        delta, w_up, (((1,), (1,)), ((), ())), preferred_element_type=jnp.float32
    )
    feature_grad = lax.psum_scatter(feature_part, "hst", scatter_dimension=1, tiled=True)
    bag_grad = feature_grad.astype(jnp.bfloat16).reshape(batch_rows, tables_dev, emb_width)
    positions = jnp.arange(bag_len, dtype=jnp.int32)
    used = positions[None, None, :] < lens[:, :, None]
    row_ids = jnp.arange(rows_dev, dtype=jnp.int32)
    marks = jnp.where(used, owners * rows_dev + rows, -1)
    my_owner = lax.axis_index("tbl")
    grads_in = lax.all_gather(bag_grad, "tbl", axis=0, tiled=True)
    weights_in = lax.all_gather(jnp.transpose(lookup_weight, (1, 0, 2)), "tbl", axis=0, tiled=True)
    marks_in = lax.all_gather(jnp.transpose(marks, (1, 0, 2)), "tbl", axis=0, tiled=True)
    is_mine = (marks_in >= 0) & (marks_in // rows_dev == my_owner)
    chosen_weight = jnp.sum(jnp.where(is_mine, weights_in.astype(jnp.float32), 0.0), axis=-1)
    chosen_row = jnp.sum(jnp.where(is_mine, marks_in - my_owner * rows_dev, 0), axis=-1)
    found_any = jnp.any(is_mine, axis=-1)
    local_row = jnp.where(found_any, chosen_row, rows_dev)
    scaled = (chosen_weight[:, :, None] * grads_in.astype(jnp.float32)).astype(jnp.bfloat16)
    placing = (jnp.transpose(local_row, (1, 0))[:, None, :] == row_ids[None, :, None]).astype(
        jnp.bfloat16
    )
    row_grad = jnp.einsum("trn,nte->tre", placing, scaled, preferred_element_type=jnp.float32)
    inverse_map = jnp.argsort(slot_map.reshape(-1))
    slot_grad = row_grad.reshape(slot_count, emb_width)[inverse_map]
    grad_up = lax.psum_scatter(
        lax.dot_general(
            pooled, delta, (((0,), (0,)), ((), ())), preferred_element_type=jnp.float32
        ),
        "tbl",
        scatter_dimension=0,
        tiled=True,
    )
    new_accum = cache_accum[0, 0] + jnp.mean(slot_grad * slot_grad, axis=-1)
    new_weight = cache_weight[0, 0] - LEARN_RATE * slot_grad / (
        jnp.sqrt(new_accum)[:, None] + EPSILON
    )
    chosen_slots = evict_slots[0, 0]
    departure = evict_dest[0, 0]
    list_len = chosen_slots.shape[0]
    hold_cap = list_len // 2
    holder_count = lax.axis_size("hst")
    leaving = new_weight[chosen_slots]
    leaving_accum = new_accum[chosen_slots]
    list_ids = jnp.arange(list_len, dtype=jnp.int32)
    live = list_ids < evict_count[0, 0]
    holder_picks = (
        (departure[:, None] == jnp.arange(holder_count, dtype=jnp.int32)) & live[:, None]
    ).astype(jnp.bfloat16)
    before = (list_ids[:, None] > list_ids[None, :]).astype(jnp.bfloat16)
    counted = jnp.dot(before, holder_picks, preferred_element_type=jnp.float32)
    placed = jnp.sum(counted * holder_picks.astype(jnp.float32), axis=-1).astype(jnp.int32)
    goal = jnp.where(live, departure * hold_cap + placed, holder_count * hold_cap)
    place_table = (
        goal[None, :] == jnp.arange(holder_count * hold_cap, dtype=jnp.int32)[:, None]
    ).astype(jnp.float32)
    send_rows = jnp.dot(
        place_table, leaving, precision=lax.Precision.HIGHEST, preferred_element_type=jnp.float32
    )
    send_accum = jnp.dot(
        place_table,
        leaving_accum,
        precision=lax.Precision.HIGHEST,
        preferred_element_type=jnp.float32,
    )
    held_rows, held_accum = (
        lax.all_to_all(
            send_rows.reshape(holder_count, hold_cap, emb_width),
            "hst",
            split_axis=0,
            concat_axis=0,
            tiled=True,
        ),
        lax.all_to_all(
            send_accum.reshape(holder_count, hold_cap),
            "hst",
            split_axis=0,
            concat_axis=0,
            tiled=True,
        ),
    )
    return (
        grad_up,
        new_weight[None, None],
        new_accum[None, None],
        held_rows[None, None],
        held_accum[None, None],
    )


def solution(mesh):
    placed = (
        P("tbl", None),
        P(None, "hst"),
        P("tbl", "hst"),
        P("hst", "tbl", None),
        P("hst", "tbl", None),
        P("hst", "tbl", None),
        P("hst", "tbl"),
        P("tbl", "hst", None),
        P("tbl", "hst", None, None),
        P("tbl", "hst", None),
        P("tbl", "hst", None),
        P("tbl", "hst", None),
        P("tbl", "hst"),
    )
    return jax.shard_map(
        on_device,
        mesh=mesh,
        in_specs=placed,
        out_specs=(
            P("tbl", "hst"),
            P("tbl", "hst", None, None),
            P("tbl", "hst", None),
            P("tbl", "hst", None, None, None),
            P("tbl", "hst", None, None),
        ),
        check_vma=False,
    )
```

profile of v0, /device:TPU:0, one launch (start us, length us, event | category | flops | bytes accessed | tf_op | source)
XLA Modules:
  0.0 178.8 jit_solution(1636801421578546220)
XLA Ops:
  7.2 1.5 copy-done
  8.8 4.0 %multiply_convert_fusion.2 = bf16[512,2048]{1,0:T(8,128)(2,1)S(1)} fusion(bf16[512,2048]{1,0:T(8,128)(2,1)} %param.15, bf16[512,512]{1,0:T(8,128)(2,1)} %param.13, bf16[512,2048]{1,0:T(8,128)(2,1)S(1)} %copy-done), kind=kOutput, calls=%fused_computation.8 | convolution fusion | flops 1084227584 | bytes 6815744 | tf_op jit(solution)/shard_map/dot_general | solution.py:29
  12.8 1.3 copy-done.2
  14.1 2.3 %fusion.17 = f32[512,512]{1,0:T(8,128)} fusion(bf16[512,2048]{1,0:T(8,128)(2,1)S(1)} %multiply_convert_fusion.2, bf16[512,2048]{1,0:T(8,128)(2,1)S(1)} %copy-done), kind=kOutput, calls=%fused_computation.51 | convolution fusion | flops 1073741824 | bytes 5242880 | tf_op jit(solution)/shard_map/dot_general | solution.py:34
  16.5 23.2 %reduce-scatter.5.cloned.1.call-done = f32[512,256]{1,0:T(8,128)} async-done(((f32[512,512]{1,0:T(8,128)}), f32[512,256]{1,0:T(8,128)}) %reduce-scatter.5.cloned.1.call-update) | async-done | bytes 524304 | tf_op jit(solution)/shard_map/reduce_scatter | solution.py:37
  39.7 1.8 copy_bitcast_fusion
  41.6 4.9 %convolution_bitcast_fusion = f32[512,2048]{0,1:T(8,128)} fusion(bf16[512,2048]{1,0:T(8,128)(2,1)} %copy-done.2, bf16[512,512]{1,0:T(8,128)(2,1)S(1)} %copy-done.3), kind=kOutput, calls=%fused_computation.9 | convolution fusion | flops 1073741824 | bytes 6815744 | tf_op jit(solution)/shard_map/dot_general | solution.py:60
  46.4 5.4 %copy.24 = f32[512,2048]{1,0:T(8,128)} copy(f32[512,2048]{0,1:T(8,128)} %convolution_bitcast_fusion) | data formatting | bytes 8388608
  52.7 23.9 %all_gather.9 = s32[8192,2,8]{0,2,1:T(8,128)S(1)} all-gather(s32[512,2,8]{0,2,1:T(8,128)S(1)} %select_bitcast_fusion.1), channel_id=1, replica_groups=mesh['tbl'=16,'hst'=2] {'tbl'}, dimensions={0}, use_global_device_ids=true | all-gather | bytes 557056 | tf_op jit(solution)/shard_map/all_gather | solution.py:46
  76.6 5.0 %sort.17 = (s32[2048]{0:T(1024)}, s32[2048]{0:T(1024)S(1)}) sort(s32[2048]{0:T(1024)S(1)} %bitcast.51, s32[2048]{0:T(1024)S(1)} %iota.30), dimensions={0}, to_apply=%region_5.6 | sort | flops 22528 | bytes 32768 | tf_op jit(solution)/shard_map/jit(argsort)/sort | solution.py:57
  81.6 18.7 %all_gather.10 = bf16[8192,2,8]{0,2,1:T(8,128)(2,1)S(1)} all-gather(bf16[512,2,8]{0,2,1:T(8,128)(2,1)S(1)} %bitcast.50), channel_id=1, replica_groups=mesh['tbl'=16,'hst'=2] {'tbl'}, dimensions={0}, use_global_device_ids=true | all-gather | bytes 278528 | tf_op jit(solution)/shard_map/all_gather | solution.py:45
  100.3 0.6 select_reduce_fusion
  100.9 0.2 reduce_or.9
  101.1 0.2 fusion.3
  101.3 0.2 select_reduce_fusion.1
  101.6 0.1 select_bitcast_fusion
  101.7 14.1 %fusion = f32[2,1024,128]{2,1,0:T(8,128)S(1)} fusion(s32[2,8192]{1,0:T(2,128)S(1)} %select_bitcast_fusion, bf16[8192,2,128]{2,0,1:T(8,128)(2,1)} %all-gather.2.cloned.1.call-done, f32[8192,2]{0,1:T(2,128)S(1)} %get-tuple-element.24), kind=kOutput, calls=%fused_computation.4 | convolution fusion | flops 4318035968 | bytes 5373952 | tf_op jit(solution)/shard_map/trn,nte->tre/dot_general | solution.py:56
  115.8 7.6 %gather_fusion = f32[2048,128]{1,0:T(8,128)} fusion(f32[2048,128]{1,0:T(8,128)S(1)} %bitcast.46, s32[2048]{0:T(1024)S(1)} %fusion.11), kind=kCustom, calls=%fused_computation | custom fusion | bytes 2105344 | tf_op jit(solution)/shard_map/gather | solution.py:58
  123.4 1.7 multiply_reduce_fusion
  125.1 1.7 gather_fusion.2
  126.9 0.8 convolution_bitcast_fusion.1
  127.7 3.2 %all-to-all-start.1 = ((f32[2,1,128]{2,1,0:T(1,128)}), f32[2,1,128]{2,1,0:T(1,128)S(1)}, u32[]{:S(2)}, u32[]{:S(2)}) async-start(f32[2,1,128]{2,1,0:T(1,128)} %convolution_bitcast_fusion.1), calls=%async_computation.2 | async-start | bytes 2048 | tf_op jit(solution)/shard_map/all_to_all | solution.py:107
  130.9 2.9 %bitcast_subtract_fusion = f32[2048,128]{1,0:T(8,128)} fusion(f32[1,1,2048,128]{3,2,1,0:T(8,128)} %param.21, f32[2048,128]{1,0:T(8,128)} %gather_fusion, f32[2048]{0:T(1024)S(1)} %get-tuple-element.22), kind=kLoop, calls=%fused_computation.13 | loop fusion | flops 786432 | bytes 3153920 | tf_op jit(solution)/shard_map/sub | solution.py:68
  133.8 2.0 %gather_fusion.1 = f32[256,128]{1,0:T(8,128)S(1)} fusion(f32[2048,128]{1,0:T(8,128)} %bitcast_subtract_fusion, s32[1024]{0:T(1024)S(1)} %pad_clamp_fusion), kind=kCustom, calls=%fused_computation.1 | custom fusion | bytes 263168 | tf_op jit(solution)/shard_map/gather | solution.py:76
  135.7 0.9 fusion.8
  136.7 3.4 %all-to-all-start = ((f32[2,128,128]{2,1,0:T(8,128)}), f32[2,128,128]{2,1,0:T(8,128)S(1)}, u32[]{:S(2)}, u32[]{:S(2)}) async-start(f32[2,128,128]{2,1,0:T(8,128)} %bitcast.14), calls=%async_computation.1 | async-start | bytes 262144 | tf_op jit(solution)/shard_map/all_to_all | solution.py:100
  140.1 2.5 %fusion.4 = f32[1,1,2048,128]{3,2,1,0:T(8,128)} fusion(f32[1,1,2048,128]{3,2,1,0:T(8,128)} %param.21, f32[2048,128]{1,0:T(8,128)S(1)} %copy-done.1, f32[2048]{0:T(1024)S(1)} %get-tuple-element.22), kind=kLoop, calls=%fused_computation.15 | loop fusion | flops 786432 | bytes 3153920 | tf_op jit(solution)/shard_map/sub | solution.py:68
  142.6 0.6 add.67
  143.2 1.4 all-to-all-done
  144.6 26.5 %reduce-scatter.7.cloned.1.call-done = f32[32,2048]{1,0:T(8,128)} async-done(((f32[512,2048]{1,0:T(8,128)}), f32[32,2048]{1,0:T(8,128)}) %reduce-scatter.7.cloned.1.call-update) | async-done | bytes 262160
  171.1 0.7 copy.31
  171.7 0.6 copy.32
  (38 shorter events, 0.3 us)
Async XLA Ops:
  7.2 1.6 copy-start
  7.2 32.5 %reduce-scatter.5.cloned.1.call-start = ((), (), s32[]{:S(2)}) async-start(), calls=%async_computation.4 | async-start | bytes 1572864 | tf_op jit(solution)/shard_map/reduce_scatter | solution.py:37
  12.8 1.3 copy-start.2
  14.1 27.4 %copy-start.3 = (bf16[512,512]{1,0:T(8,128)(2,1)S(1)}, bf16[512,512]{1,0:T(8,128)(2,1)}, u32[]{:S(2)}) copy-start(bf16[512,512]{1,0:T(8,128)(2,1)} %param.13) | copy-start | bytes 1572868
  16.4 85.2 %all-gather.2.cloned.1.call-start = ((), (), s32[]{:S(2)}) async-start(), calls=%async_computation.5 | async-start | bytes 4456448 | tf_op jit(solution)/shard_map/all_gather | solution.py:44
  41.5 129.6 %reduce-scatter.7.cloned.1.call-start = ((), (), s32[]{:S(2)}) async-start(), calls=%async_computation.6 | async-start | bytes 4456448
  51.8 0.8 copy-start.4
  51.8 0.8 copy-start.5
  51.8 0.8 copy-start.9
  51.8 24.7 %copy-start.8 = (s32[1,1,2048]{2,1,0:T(1,128)S(1)}, s32[1,1,2048]{2,1,0:T(1,128)}, u32[]{:S(2)}) copy-start(s32[1,1,2048]{2,1,0:T(1,128)} %param.20) | copy-start | bytes 24580
  51.9 29.7 %copy-start.7 = (bf16[2,512,8]{1,2,0:T(8,128)(2,1)S(1)}, bf16[2,512,8]{1,2,0:T(8,128)(2,1)}, u32[]{:S(2)}) copy-start(bf16[2,512,8]{1,2,0:T(8,128)(2,1)} %param.18) | copy-start | bytes 49156
  51.9 49.2 %copy-start.11 = (s32[1,1,256]{2,1,0:T(1,128)S(1)}, s32[1,1,256]{2,1,0:T(1,128)}, u32[]{:S(2)}) copy-start(s32[1,1,256]{2,1,0:T(1,128)} %param.23) | copy-start | bytes 3076
  51.9 49.2 %copy-start.10 = (s32[1,1,256]{2,1,0:T(1,128)S(1)}, s32[1,1,256]{2,1,0:T(1,128)}, u32[]{:S(2)}) copy-start(s32[1,1,256]{2,1,0:T(1,128)} %param.24) | copy-start | bytes 3076
  115.8 9.3 %copy-start.6 = (f32[1,1,2048]{2,1,0:T(1,128)S(1)}, f32[1,1,2048]{2,1,0:T(1,128)}, u32[]{:S(2)}) copy-start(f32[1,1,2048]{2,1,0:T(1,128)} %param.22) | copy-start | bytes 24580
  123.4 16.6 %copy-start.1 = (f32[2048,128]{1,0:T(8,128)S(1)}, f32[2048,128]{1,0:T(8,128)}, u32[]{:S(2)}) copy-start(f32[2048,128]{1,0:T(8,128)} %gather_fusion) | copy-start | bytes 3145732
  127.7 9.0 %all-to-all-start.1 = ((f32[2,1,128]{2,1,0:T(1,128)}), f32[2,1,128]{2,1,0:T(1,128)S(1)}, u32[]{:S(2)}, u32[]{:S(2)}) async-start(f32[2,1,128]{2,1,0:T(1,128)} %convolution_bitcast_fusion.1), calls=%async_computation.2 | async-start | bytes 2048 | tf_op jit(solution)/shard_map/all_to_all | solution.py:107
  136.7 7.9 %all-to-all-start = ((f32[2,128,128]{2,1,0:T(8,128)}), f32[2,128,128]{2,1,0:T(8,128)S(1)}, u32[]{:S(2)}, u32[]{:S(2)}) async-start(f32[2,128,128]{2,1,0:T(8,128)} %bitcast.14), calls=%async_computation.1 | async-start | bytes 262144 | tf_op jit(solution)/shard_map/all_to_all | solution.py:100
Sparse Core Ops, SparseCore 0:
  16.5 23.1 reduce-scatter.4
  42.5 52.0 all-gather.1
  99.0 72.0 reduce-scatter.6
where the time goes:
time: 180 us; the launch traced here: 179 us
  waiting for transfers between devices  51.2 us (28%)
  blocking collectives  42.6 us (24%)
  matrix products  27.2 us (15%)
  local copies, waits for them, and re-layouts  20.9 us (12%)
  other arithmetic  15.6 us (9%)
  between operations  14.7 us (8%)
  starting transfers between devices  6.7 us (4%)
    unnamed x4, waiting for transfers between devices  26.6 us
    all_gather x1, blocking collectives, on_device(): lax.all_gather(jnp.transpose(marks, (1, 0, 2)), 'tbl', axis=0, tiled=True)  23.9 us
    reduce_scatter x1, waiting for transfers between devices, on_device(): lax.psum_scatter(feature_part, 'hst', scatter_dimension=1, tiled=True)  23.2 us
    all_gather x1, blocking collectives, on_device(): lax.all_gather(jnp.transpose(lookup_weight, (1, 0, 2)), 'tbl', axis=0, ti...  18.7 us
    dot_general x1, matrix products, on_device(): jnp.einsum('trn,nte->tre', placing, scaled, preferred_element_type=jnp.fl...  14.1 us
    unnamed x27, local copies, waits for them, and re-layouts  9.55 us
    gather x1, local copies, waits for them, and re-layouts, on_device(): slot_grad = row_grad.reshape(slot_count, emb_width)[inverse_map]  7.64 us
    sub x2, other arithmetic, on_device(): cache_weight[0, 0]  5.42 us
  transfers between devices with their start and end apart: 5, of which 3 were waited for; matrix products, arithmetic and copies ran while one was open for 29% of the time, Pallas kernels for 0%

commit v1 on v0

v1 whole, which is shorter than its diff:
```python
import functools

import jax
import jax.numpy as jnp
from jax import lax
from jax.experimental import pallas as pl
from jax.experimental.pallas import tpu as pltpu
from jax.sharding import PartitionSpec as P

LEARN_RATE = 0.05
EPSILON = 1e-08
MESH = pl.DeviceIdType.MESH
F32 = jnp.float32
BF16 = jnp.bfloat16


def exchange_kernel(
    nz, nx, nh, tables, rows_dev,
    feat, grad, idx,
    grad_out_ref, place_ref,
    ybuf, gat, idxb, rcore, a1, rx, a2, rz,
    y_s, y_r, i_s, i_r, az_s, ax_s, ac_s, g_r, rc_s, rc_r, rx_s, rx_r, rz_s, rz_r,
):
    n = nz * nx * 2
    me = lax.axis_index("tbl")
    h = lax.axis_index("hst")
    c = lax.rem(me, 2)
    zx = me // 2
    x = lax.rem(zx, nx)
    z = zx // nx
    other = 1 - c
    width = ybuf.shape[-1]
    emb = width // tables

    def at(zi, xi, ci):
        return (zi * nx + xi) * 2 + ci

    def zof(d):
        return lax.rem(z + d, nz)

    def xof(d):
        return lax.rem(x + d, nx)

    def rcopy(src, dst, s, r, dev):
        return pltpu.make_async_remote_copy(
            src_ref=src, dst_ref=dst, send_sem=s, recv_sem=r,
            device_id=dev, device_id_type=MESH,
        )

    barrier = pltpu.get_barrier_semaphore()

    def greet(d, carry):
        pl.semaphore_signal(
            barrier, inc=1, device_id={"tbl": lax.rem(me + d, n)}, device_id_type=MESH
        )
        return carry

    lax.fori_loop(1, n, greet, 0)
    for d in range(1, nh):
        pl.semaphore_signal(
            barrier, inc=1, device_id={"hst": lax.rem(h + d, nh)}, device_id_type=MESH
        )
    pl.semaphore_wait(barrier, n - 1 + nh - 1)

    def cols(hh):
        return pl.ds(pl.multiple_of(hh * width, width), width)

    def y_copy(d):
        h2 = lax.rem(h + d, nh)
        return rcopy(feat.at[:, cols(h2)], ybuf.at[h], y_s.at[d], y_r.at[h], {"hst": h2})

    def y_arrival(d):
        h2 = lax.rem(h + d, nh)
        return rcopy(feat.at[:, cols(h2)], ybuf.at[h2], y_s.at[d], y_r.at[h2], {"hst": h2})

    def core_copy(x2):
        return rcopy(
            grad.at[:, x2, other], rcore.at[:, x2], rc_s.at[x2], rc_r.at[x2],
            {"tbl": at(z, x, other)},
        )

    def i_copy(d):
        o = lax.rem(me + d, n)
        return rcopy(idx.at[o], idxb.at[me], i_s.at[d], i_r.at[me], {"tbl": o})

    def i_arrival(slot):
        return rcopy(idx.at[slot], idxb.at[slot], i_s.at[0], i_r.at[slot], {"tbl": at(z, x, other)})

    for d in range(1, nh):
        y_copy(d).start()
    for d in range(1, nx + 1):
        core_copy(xof(d)).start()

    def i_start(d, carry):
        i_copy(d).start()
        return carry

    lax.fori_loop(1, n, i_start, 0)

    def rx_copy(d):
        x2 = xof(d)
        return rcopy(a1.at[:, x2], rx.at[x], rx_s.at[x2], rx_r.at[x], {"tbl": at(z, x2, c)})

    def rx_arrival(d):
        x2 = xof(d)
        return rcopy(a1.at[:, x2], rx.at[x2], rx_s.at[x2], rx_r.at[x2], {"tbl": at(z, x2, c)})

    for d in range(1, nx):
        x2 = xof(d)
        core_copy(x2).wait_recv()

        def add_core(k, carry):
            a1[k, x2] = (grad[k, x2, c].astype(F32) + rcore[k, x2].astype(F32)).astype(BF16)
            return carry

        lax.fori_loop(0, nz, add_core, 0)
        rx_copy(d).start()

    for d in range(1, nh):
        y_arrival(d).wait_recv()
    total = feat[:, cols(h)].astype(F32)
    for d in range(1, nh):
        total = total + ybuf[lax.rem(h + d, nh)].astype(F32)
    gat[me] = total.astype(BF16)

    def g_copy(slot, sem, dev):
        return rcopy(gat.at[slot], gat.at[slot], sem, g_r.at[slot], {"tbl": dev})

    def z_copy(d):
        return g_copy(me, az_s.at[d], at(zof(d), x, c))

    def x_copy(zi, d):
        return g_copy(at(zi, x, c), ax_s.at[zi, d], at(z, xof(d), c))

    def c_copy(zi, xi):
        return g_copy(at(zi, xi, c), ac_s.at[zi, xi], at(z, x, other))

    def arrived(slot):
        g_copy(slot, ac_s.at[0, 0], at(z, x, other)).wait_recv()

    for d in range(1, nx):
        x_copy(z, d).start()

    def z_start(d, carry):
        z_copy(d).start()
        return carry

    lax.fori_loop(1, nz, z_start, 0)
    c_copy(z, x).start()

    place_ref[...] = jnp.zeros_like(place_ref)
    idxb[me] = idx[me]
    chunk = min(256, rows_dev)
    batch = gat.shape[1]

    def proc(slot):
        meta = idxb[slot]
        block = gat[slot]
        for t in range(tables):
            row = meta[t : t + 1, :]
            wgt = meta[tables + t : tables + t + 1, :]
            part = block[:, t * emb : (t + 1) * emb]
            for r0 in range(0, rows_dev, chunk):
                ids = lax.broadcasted_iota(jnp.int32, (chunk, batch), 0).astype(F32) + float(r0)
                mark = jnp.where(ids == row, wgt, 0.0).astype(BF16)
                place_ref[pl.ds(t * rows_dev + r0, chunk), :] += jnp.dot(
                    mark, part, preferred_element_type=F32
                )

    proc(me)

    def z_body(d, carry):
        zi = zof(d)
        slot = at(zi, x, c)
        arrived(slot)
        for dx in range(1, nx):
            x_copy(zi, dx).start()
        c_copy(zi, x).start()
        i_arrival(slot).wait_recv()
        proc(slot)
        return carry

    lax.fori_loop(1, nz, z_body, 0)

    core_copy(x).wait_recv()
    for d in range(1, nx):
        rx_arrival(d).wait_recv()

    def own_sum(k):
        s = grad[k, x, c].astype(F32) + rcore[k, x].astype(F32)
        for d in range(1, nx):
            s = s + rx[xof(d), k].astype(F32)
        return s

    def rz_copy(d):
        zi = zof(d)
        return rcopy(a2.at[zi], rz.at[z], rz_s.at[d], rz_r.at[z], {"tbl": at(zi, x, c)})

    def rz_arrival(d):
        zi = zof(d)
        return rcopy(a2.at[zi], rz.at[zi], rz_s.at[d], rz_r.at[zi], {"tbl": at(zi, x, c)})

    def rz_start(d, carry):
        zi = zof(d)
        a2[zi] = own_sum(zi).astype(BF16)
        rz_copy(d).start()
        return carry

    lax.fori_loop(1, nz, rz_start, 0)

    def x_body(k, carry):
        zi = zof(k // (nx - 1))
        xi = xof(1 + lax.rem(k, nx - 1))
        slot = at(zi, xi, c)
        arrived(slot)
        c_copy(zi, xi).start()
        i_arrival(slot).wait_recv()
        proc(slot)
        return carry

    if nx > 1:
        lax.fori_loop(0, nz * (nx - 1), x_body, 0)

    def c_body(k, carry):
        j = k // nz
        zi = zof(lax.rem(k, nz))
        slot = at(zi, xof(j), other)
        arrived(slot)
        i_arrival(slot).wait_recv()
        proc(slot)
        return carry

    lax.fori_loop(0, nz * nx, c_body, 0)

    grad_out_ref[...] = own_sum(z)

    def rz_end(d, carry):
        rz_arrival(d).wait_recv()
        grad_out_ref[...] += rz[zof(d)].astype(F32)
        return carry

    lax.fori_loop(1, nz, rz_end, 0)

    for d in range(1, nh):
        y_copy(d).wait_send()
    for d in range(1, nx + 1):
        core_copy(xof(d)).wait_send()
    for d in range(1, nx):
        rx_copy(d).wait_send()

    def i_end(d, carry):
        i_copy(d).wait_send()
        return carry

    lax.fori_loop(1, n, i_end, 0)

    def z_end(d, carry):
        z_copy(d).wait_send()
        rz_copy(d).wait_send()
        return carry

    lax.fori_loop(1, nz, z_end, 0)

    def end_all(k, carry):
        for dx in range(1, nx):
            x_copy(k, dx).wait_send()
        for xi in range(nx):
            c_copy(k, xi).wait_send()
        return carry

    lax.fori_loop(0, nz, end_all, 0)


def update_kernel(
    slot_map, evict_slots, goal, place, weight, accum,
    new_weight, new_accum, send_rows, send_accum,
    sgrad, wide,
):
    slots = place.shape[0]
    list_len = evict_slots.shape[0]
    keep = send_accum.shape[0] * send_accum.shape[1]
    step = 16

    def scatter(i, carry):
        for j in range(step):
            r = i * step + j
            sgrad[pl.ds(slot_map[r], 1), :] = place[pl.ds(r, 1), :]
        return carry

    lax.fori_loop(0, slots // step, scatter, 0)
    tile = 128

    def adagrad(i, carry):
        at = pl.ds(i * tile, tile)
        g = sgrad[at, :]
        acc = accum[pl.ds(i, 1), :] + jnp.mean(g * g, axis=-1)[None, :]
        new_accum[pl.ds(i, 1), :] = acc
        col = jnp.broadcast_to(acc.reshape(tile, 1), g.shape)
        wide[at, :] = col
        new_weight[at, :] = weight[at, :] - LEARN_RATE * g / (jnp.sqrt(col) + EPSILON)
        return carry

    lax.fori_loop(0, slots // tile, adagrad, 0)
    send_rows[...] = jnp.zeros_like(send_rows)
    sgrad[...] = jnp.zeros_like(sgrad)

    def evict(i, carry):
        for j in range(8):
            p = i * 8 + j
            s = evict_slots[p]
            k = goal[p]
            send_rows[pl.ds(k, 1), :] = new_weight[pl.ds(s, 1), :]
            sgrad[pl.ds(k, 1), :] = wide[pl.ds(s, 1), :]
        return carry

    lax.fori_loop(0, list_len // 8, evict, 0)
    groups = send_accum.shape[0]
    cap = keep // groups
    for d in range(groups):
        send_accum[d : d + 1, :] = jnp.max(sgrad[d * cap : (d + 1) * cap, :], axis=-1)[None, :]


def on_device(
    nz, nx,
    pooled, w_up, grad_out, owners, rows, lookup_weight, lens, slot_map,
    cache_weight, cache_accum, evict_slots, evict_dest, evict_count,
):
    tables, batch, bag_len = owners.shape
    slots = slot_map.shape[-1]
    rows_dev = slots // tables
    emb = cache_weight.shape[-1]
    n = lax.axis_size("tbl")
    nh = lax.axis_size("hst")
    feat_n, hid = w_up.shape
    out_rows = feat_n // n
    width = tables * emb

    preact = jnp.dot(pooled, w_up, preferred_element_type=F32)
    sig = jax.nn.sigmoid(preact)
    delta = (grad_out.astype(F32) * sig * (1.0 + preact * (1.0 - sig))).astype(BF16)
    feat = lax.dot_general(
        delta, w_up, (((1,), (1,)), ((), ())), preferred_element_type=F32
    ).astype(BF16)
    grad = lax.dot_general(
        pooled, delta, (((0,), (0,)), ((), ())), preferred_element_type=F32
    ).astype(BF16)
    grad = grad.reshape(nz, nx, 2, out_rows, hid)

    own_t = jnp.transpose(owners, (2, 0, 1))
    row_t = jnp.transpose(rows, (2, 0, 1)).astype(F32)
    wgt_t = jnp.transpose(lookup_weight, (2, 0, 1)).astype(F32)
    used = jnp.arange(bag_len, dtype=jnp.int32)[:, None, None] < lens[None]
    hit = (own_t[None] == jnp.arange(n, dtype=jnp.int32)[:, None, None, None]) & used[None]
    row_to = jnp.sum(jnp.where(hit, row_t[None] + 1.0, 0.0), axis=1) - 1.0
    wgt_to = jnp.sum(jnp.where(hit, wgt_t[None], 0.0), axis=1)
    idx = jnp.concatenate([row_to, wgt_to], axis=1)

    dma = pltpu.SemaphoreType.DMA
    vmem = pl.BlockSpec(memory_space=pltpu.VMEM)
    smem = pl.BlockSpec(memory_space=pltpu.SMEM)
    grad_up, place = pl.pallas_call(
        functools.partial(exchange_kernel, nz, nx, nh, tables, rows_dev),
        out_shape=(
            jax.ShapeDtypeStruct((out_rows, hid), F32),
            jax.ShapeDtypeStruct((slots, emb), F32),
        ),
        in_specs=[vmem] * 3,
        out_specs=(vmem, vmem),
        scratch_shapes=[
            pltpu.VMEM((nh, batch, width), BF16),
            pltpu.VMEM((n, batch, width), BF16),
            pltpu.VMEM((n, 2 * tables, batch), F32),
            pltpu.VMEM((nz, nx, out_rows, hid), BF16),
            pltpu.VMEM((nz, nx, out_rows, hid), BF16),
            pltpu.VMEM((nx, nz, out_rows, hid), BF16),
            pltpu.VMEM((nz, out_rows, hid), BF16),
            pltpu.VMEM((nz, out_rows, hid), BF16),
            dma((nh,)), dma((nh,)), dma((n,)), dma((n,)),
            dma((nz,)), dma((nz, nx)), dma((nz, nx)), dma((n,)),
            dma((nx,)), dma((nx,)), dma((nx,)), dma((nx,)), dma((nz,)), dma((nz,)),
        ],
        compiler_params=pltpu.CompilerParams(
            collective_id=0, has_side_effects=True, vmem_limit_bytes=60 * 1024 * 1024
        ),
        name="exchange",
    )(feat, grad, idx)

    chosen = evict_slots[0, 0]
    dest = evict_dest[0, 0]
    list_len = chosen.shape[0]
    cap = list_len // 2
    ids = jnp.arange(list_len, dtype=jnp.int32)
    live = ids < evict_count[0, 0]
    same = (dest[:, None] == dest[None, :]) & (ids[:, None] > ids[None, :]) & live[None, :]
    goal = jnp.where(live, dest * cap + jnp.sum(same.astype(jnp.int32), axis=1), nh * cap)

    new_weight, new_accum, send_rows, send_accum = pl.pallas_call(
        update_kernel,
        out_shape=(
            jax.ShapeDtypeStruct((slots, emb), F32),
            jax.ShapeDtypeStruct((slots // 128, 128), F32),
            jax.ShapeDtypeStruct((nh * cap + 8, emb), F32),
            jax.ShapeDtypeStruct((nh, cap), F32),
        ),
        in_specs=[smem] * 3 + [vmem] * 3,
        out_specs=(vmem,) * 4,
        scratch_shapes=[pltpu.VMEM((slots, emb), F32), pltpu.VMEM((slots, emb), F32)],
        name="update",
    )(
        slot_map.reshape(slots), chosen, goal.astype(jnp.int32), place,
        cache_weight.reshape(slots, emb), cache_accum.reshape(slots // 128, 128),
    )
    pad = -(-cap // emb)
    both = jnp.concatenate(
        [send_rows[: nh * cap].reshape(nh, cap, emb), send_accum.reshape(nh, pad, emb)], axis=1
    )
    both = lax.all_to_all(both, "hst", split_axis=0, concat_axis=0, tiled=True)
    return (
        grad_up,
        new_weight[None, None],
        new_accum.reshape(1, 1, slots),
        both[:, :cap][None, None],
        both[:, cap:].reshape(1, 1, nh, cap),
    )


def solution(mesh):
    n, nh = mesh.shape["tbl"], mesh.shape["hst"]
    nx = nh if n % (2 * nh) == 0 else 1
    nz = n // (2 * nx)
    placed = (
        P("tbl", None),
        P(None, "hst"),
        P("tbl", "hst"),
        P("hst", "tbl", None),
        P("hst", "tbl", None),
        P("hst", "tbl", None),
        P("hst", "tbl"),
        P("tbl", "hst", None),
        P("tbl", "hst", None, None),
        P("tbl", "hst", None),
        P("tbl", "hst", None),
        P("tbl", "hst", None),
        P("tbl", "hst"),
    )
    return jax.shard_map(
        functools.partial(on_device, nz, nx),
        mesh=mesh,
        in_specs=placed,
        out_specs=(
            P("tbl", "hst"),
            P("tbl", "hst", None, None),
            P("tbl", "hst", None),
            P("tbl", "hst", None, None, None),
            P("tbl", "hst", None, None),
        ),
        check_vma=False,
    )
```

time: 180 us -> 98.6 us (0.55)
  the two profiles are of different devices: /device:TPU:0 before, /device:TPU:10 now
where the time goes in v1:
time: 98.6 us; the launch traced here: 98.2 us
  Pallas kernels  72.4 us (73%)
  matrix products  8.78 us (9%)
  waiting for transfers between devices  4.5 us (5%)
  local copies, waits for them, and re-layouts  4.47 us (5%)
  starting transfers between devices  3.42 us (3%)
  other arithmetic  3.29 us (3%)
  between operations  1.42 us (1%)
    pallas_call x1, Pallas kernels, on_device(): pl.pallas_call(functools.partial(exchange_kernel, nz, nx, nh, tables, row...  63.6 us
    pallas_call x1, Pallas kernels, on_device(): pl.pallas_call(update_kernel, out_shape=(jax.ShapeDtypeStruct((slots, emb...  8.76 us
    all_to_all x1, waiting for transfers between devices, on_device(): both = lax.all_to_all(both, 'hst', split_axis=0, concat_axis=0, tiled=True)  4.5 us
    dot_general x1, matrix products, on_device(): preact = jnp.dot(pooled, w_up, preferred_element_type=F32)  4.03 us
    all_to_all x1, starting transfers between devices, on_device(): both = lax.all_to_all(both, 'hst', split_axis=0, concat_axis=0, tiled=True)  3.42 us
    dot_general x1, matrix products, on_device(): lax.dot_general(pooled, delta, (((0,), (0,)), ((), ())), preferred_elemen...  2.66 us
    unnamed x17, local copies, waits for them, and re-layouts  2.33 us
    dot_general x1, matrix products, on_device(): lax.dot_general(delta, w_up, (((1,), (1,)), ((), ())), preferred_element_...  2.09 us
  transfers between devices with their start and end apart: 1, of which 1 were waited for; matrix products, arithmetic and copies ran while one was open for 0% of the time, Pallas kernels for 0%

profile of v1, /device:TPU:10, one launch (start us, length us, event | category | flops | bytes accessed | tf_op | source)
XLA Modules:
  0.0 98.2 jit_solution(5619690917132056999)
XLA Ops:
  0.6 0.0 copy-start
  0.6 1.6 %copy-done = bf16[512,2048]{1,0:T(8,128)(2,1)S(1)} copy-done((bf16[512,2048]{1,0:T(8,128)(2,1)S(1)}, bf16[512,2048]{1,0:T(8,128)(2,1)}, u32[]{:S(2)}) %copy-start) | copy-done | bytes 2097176
  2.2 4.0 %multiply_convert_fusion = bf16[512,2048]{1,0:T(8,128)(2,1)S(1)} fusion(bf16[512,2048]{1,0:T(8,128)(2,1)} %param.15, bf16[512,512]{1,0:T(8,128)(2,1)} %param.13, bf16[512,2048]{1,0:T(8,128)(2,1)S(1)} %copy-done), kind=kOutput, calls=%fused_computation | convolution fusion | flops 1084227584 | bytes 6815744 | tf_op jit(solution)/shard_map/dot_general | solution.py:338
  6.3 0.0 copy-start.7
  6.3 2.1 %convolution_convert_fusion.1.feat = bf16[512,512]{1,0:T(8,128)(2,1)} fusion(bf16[512,2048]{1,0:T(8,128)(2,1)S(1)} %multiply_convert_fusion, bf16[512,2048]{1,0:T(8,128)(2,1)S(1)} %copy-done), kind=kOutput, calls=%fused_computation.2 | convolution fusion | flops 1074003968 | bytes 4718592 | tf_op jit(solution)/shard_map/dot_general | solution.py:341
  8.4 0.0 copy-done.7
  8.4 0.0 copy-start.2
  8.4 0.0 copy-start.6
  8.4 0.0 copy-start.4
  8.4 0.0 copy-start.3
  8.4 0.0 copy-start.5
  8.4 2.7 %convolution_convert_fusion = bf16[2048,512]{0,1:T(8,128)(2,1)} fusion(bf16[512,2048]{1,0:T(8,128)(2,1)S(1)} %multiply_convert_fusion, bf16[512,512]{1,0:T(8,128)(2,1)S(1)} %copy-done.7), kind=kOutput, calls=%fused_computation.1 | convolution fusion | flops 1074790400 | bytes 4718592 | tf_op jit(solution)/shard_map/dot_general | solution.py:344
  11.1 0.0 copy-done.2
  11.1 0.0 copy-done.6
  11.1 0.0 copy-done.4
  11.1 0.0 copy-done.3
  11.1 0.4 select_reduce_fusion.1
  12.2 0.7 pad_maximum_fusion.1.idx
  13.0 0.0 copy-done.5
  13.0 0.2 convert_reduce_fusion
  13.2 0.6 add_select_fusion.goal
  13.7 63.6 %exchange.1 = (f32[32,2048]{1,0:T(8,128)}, f32[2048,128]{1,0:T(8,128)}) custom-call(bf16[512,512]{1,0:T(8,128)(2,1)} %convolution_convert_fusion.1.feat, bf16[4,2,2,32,2048]{4,3,2,1,0:T(8,128)(2,1)} %bitcast.31, f32[16,4,512]{2,1,0:T(4,128)} %pad_maximum_fusion.1.idx), custom_call_target="tpu_custom_call" | custom-call | tf_op jit(solution)/shard_map/exchange/pallas_call | solution.py:361
  77.3 0.0 copy-start.1
  77.4 8.8 %update.1 = (f32[2048,128]{1,0:T(8,128)}, f32[16,128]{1,0:T(8,128)}, f32[264,128]{1,0:T(8,128)}, f32[2,128]{1,0:T(2,128)}) custom-call(s32[2048]{0:T(1024)} %bitcast.37, s32[256]{0:T(256)} %bitcast.39, s32[256]{0:T(256)} %add_select_fusion.goal, f32[2048,128]{1,0:T(8,128)} %get-tuple-element.12.place, f32[2048,128]{1,0:T(8,128)} %bitcast.32, f32[16,128]{1,0:T(8,128)} %bitcast.38), custom_call_target="tpu_custom_call" | custom-call | tf_op jit(solution)/shard_map/update/pallas_call | solution.py:397
  86.1 0.9 slice.9
  87.0 1.3 %pad_maximum_fusion = f32[2,129,128]{2,1,0:T(8,128)} fusion(f32[2,1,128]{2,1,0:T(1,128)} %bitcast.40, f32[2,128,128]{2,1,0:T(8,128)S(1)} %bitcast.33), kind=kLoop, calls=%fused_computation.11 | loop fusion | flops 33024 | bytes 264192 | tf_op jit(solution)/shard_map/concatenate | solution.py:414
  88.4 3.4 %all-to-all-start = ((f32[2,129,128]{2,1,0:T(8,128)}), f32[2,129,128]{2,1,0:T(8,128)S(1)}, u32[]{:S(2)}, u32[]{:S(2)}) async-start(f32[2,129,128]{2,1,0:T(8,128)} %pad_maximum_fusion), calls=%async_computation | async-start | bytes 278528 | tf_op jit(solution)/shard_map/all_to_all | solution.py:417
  91.8 4.5 %all-to-all-done = f32[2,129,128]{2,1,0:T(8,128)S(1)} async-done(((f32[2,129,128]{2,1,0:T(8,128)}), f32[2,129,128]{2,1,0:T(8,128)S(1)}, u32[]{:S(2)}, u32[]{:S(2)}) %all-to-all-start) | async-done | bytes 132128 | tf_op jit(solution)/shard_map/all_to_all | solution.py:417
  96.3 0.7 slice_bitcast_fusion
  97.0 0.6 slice.13
  97.5 0.0 copy-done.1
  97.5 0.7 copy.29
  (5 shorter events, 0.1 us)
Async XLA Ops:
  0.6 1.6 %copy-start = (bf16[512,2048]{1,0:T(8,128)(2,1)S(1)}, bf16[512,2048]{1,0:T(8,128)(2,1)}, u32[]{:S(2)}) copy-start(bf16[512,2048]{1,0:T(8,128)(2,1)} %param.14) | copy-start | bytes 6291460
  6.3 2.1 %copy-start.7 = (bf16[512,512]{1,0:T(8,128)(2,1)S(1)}, bf16[512,512]{1,0:T(8,128)(2,1)}, u32[]{:S(2)}) copy-start(bf16[512,512]{1,0:T(8,128)(2,1)} %param.13) | copy-start | bytes 1572868
  8.4 2.7 %copy-start.2 = (s32[2,512,8]{1,2,0:T(8,128)S(1)}, s32[2,512,8]{1,2,0:T(8,128)}, u32[]{:S(2)}) copy-start(s32[2,512,8]{1,2,0:T(8,128)} %param.17) | copy-start | bytes 98308
  8.4 2.7 %copy-start.6 = (s32[2,512]{1,0:T(2,128)S(1)}, s32[2,512]{1,0:T(2,128)}, u32[]{:S(2)}) copy-start(s32[2,512]{1,0:T(2,128)} %param.19) | copy-start | bytes 12292
  8.4 2.7 %copy-start.4 = (bf16[2,512,8]{1,2,0:T(8,128)(2,1)S(1)}, bf16[2,512,8]{1,2,0:T(8,128)(2,1)}, u32[]{:S(2)}) copy-start(bf16[2,512,8]{1,2,0:T(8,128)(2,1)} %param.18) | copy-start | bytes 49156
  8.4 2.7 %copy-start.3 = (s32[2,512,8]{1,2,0:T(8,128)S(1)}, s32[2,512,8]{1,2,0:T(8,128)}, u32[]{:S(2)}) copy-start(s32[2,512,8]{1,2,0:T(8,128)} %param.16) | copy-start | bytes 98308
  8.4 4.6 %copy-start.5 = (s32[1,1,256]{2,1,0:T(1,128)S(1)}, s32[1,1,256]{2,1,0:T(1,128)}, u32[]{:S(2)}) copy-start(s32[1,1,256]{2,1,0:T(1,128)} %param.24) | copy-start | bytes 3076
  77.3 20.2 %copy-start.1 = (f32[32,2048]{1,0:T(8,128)S(1)}, f32[32,2048]{1,0:T(8,128)}, u32[]{:S(2)}) copy-start(f32[32,2048]{1,0:T(8,128)} %get-tuple-element.24) | copy-start | bytes 786436
  88.4 7.9 %all-to-all-start = ((f32[2,129,128]{2,1,0:T(8,128)}), f32[2,129,128]{2,1,0:T(8,128)S(1)}, u32[]{:S(2)}, u32[]{:S(2)}) async-start(f32[2,129,128]{2,1,0:T(8,128)} %pad_maximum_fusion), calls=%async_computation | async-start | bytes 278528 | tf_op jit(solution)/shard_map/all_to_all | solution.py:417

commit v2 on v1

--- a/solution.py
+++ b/solution.py
@@ -10,6 +10,7 @@
 LEARN_RATE = 0.05
 EPSILON = 1e-08
 MESH = pl.DeviceIdType.MESH
+PIECES = 2
 F32 = jnp.float32
 BF16 = jnp.bfloat16
 
@@ -19,7 +20,7 @@
     feat, grad, idx,
     grad_out_ref, place_ref,
     ybuf, gat, idxb, rcore, a1, rx, a2, rz,
-    y_s, y_r, i_s, i_r, az_s, ax_s, ac_s, g_r, rc_s, rc_r, rx_s, rx_r, rz_s, rz_r,
+    y_s, y_r, i_s, i_r, azr_s, azl_s, ax_s, ac_s, g_r, rc_s, rc_r, rx_s, rx_r, rz_s, rz_r,
 ):
     n = nz * nx * 2
     me = lax.axis_index("tbl")
@@ -65,13 +66,24 @@
     def cols(hh):
         return pl.ds(pl.multiple_of(hh * width, width), width)
 
-    def y_copy(d):
+    batch = gat.shape[1]
+    piece = batch // PIECES
+
+    def span(k):
+        return pl.ds(k * piece, piece)
+
+    def y_copy(d, k):
         h2 = lax.rem(h + d, nh)
-        return rcopy(feat.at[:, cols(h2)], ybuf.at[h], y_s.at[d], y_r.at[h], {"hst": h2})
-
-    def y_arrival(d):
+        return rcopy(
+            feat.at[span(k), cols(h2)], ybuf.at[h, span(k)], y_s.at[d, k], y_r.at[h, k], {"hst": h2}
+        )
+
+    def y_arrival(d, k):
         h2 = lax.rem(h + d, nh)
-        return rcopy(feat.at[:, cols(h2)], ybuf.at[h2], y_s.at[d], y_r.at[h2], {"hst": h2})
+        return rcopy(
+            feat.at[span(k), cols(h2)], ybuf.at[h2, span(k)], y_s.at[d, k], y_r.at[h2, k],
+            {"hst": h2},
+        )
 
     def core_copy(x2):
         return rcopy(
@@ -86,8 +98,9 @@
     def i_arrival(slot):
         return rcopy(idx.at[slot], idxb.at[slot], i_s.at[0], i_r.at[slot], {"tbl": at(z, x, other)})
 
-    for d in range(1, nh):
-        y_copy(d).start()
+    for k in range(PIECES):
+        for d in range(1, nh):
+            y_copy(d, k).start()
     for d in range(1, nx + 1):
         core_copy(xof(d)).start()
 
@@ -110,48 +123,54 @@
         core_copy(x2).wait_recv()
 
         def add_core(k, carry):
-            a1[k, x2] = (grad[k, x2, c].astype(F32) + rcore[k, x2].astype(F32)).astype(BF16)
+            a1[k, x2] = (grad[k, x2, c] + rcore[k, x2]).astype(BF16)
             return carry
 
         lax.fori_loop(0, nz, add_core, 0)
         rx_copy(d).start()
 
-    for d in range(1, nh):
-        y_arrival(d).wait_recv()
-    total = feat[:, cols(h)].astype(F32)
-    for d in range(1, nh):
-        total = total + ybuf[lax.rem(h + d, nh)].astype(F32)
-    gat[me] = total.astype(BF16)
-
-    def g_copy(slot, sem, dev):
-        return rcopy(gat.at[slot], gat.at[slot], sem, g_r.at[slot], {"tbl": dev})
-
-    def z_copy(d):
-        return g_copy(me, az_s.at[d], at(zof(d), x, c))
-
-    def x_copy(zi, d):
-        return g_copy(at(zi, x, c), ax_s.at[zi, d], at(z, xof(d), c))
-
-    def c_copy(zi, xi):
-        return g_copy(at(zi, xi, c), ac_s.at[zi, xi], at(z, x, other))
-
-    def arrived(slot):
-        g_copy(slot, ac_s.at[0, 0], at(z, x, other)).wait_recv()
-
-    for d in range(1, nx):
-        x_copy(z, d).start()
-
-    def z_start(d, carry):
-        z_copy(d).start()
-        return carry
-
-    lax.fori_loop(1, nz, z_start, 0)
-    c_copy(z, x).start()
+    def g_copy(slot, k, sem, dev):
+        ref = gat.at[slot, span(k)]
+        return rcopy(ref, ref, sem, g_r.at[slot, k], {"tbl": dev})
+
+    def right_copy(zi, k):
+        return g_copy(at(zi, x, c), k, azr_s.at[zi, k], at(z + 1, x, c))
+
+    def left_copy(zi, k):
+        return g_copy(at(zi, x, c), k, azl_s.at[zi, k], at(z - 1, x, c))
+
+    def x_copy(zi, d, k):
+        return g_copy(at(zi, x, c), k, ax_s.at[zi, d, k], at(z, xof(d), c))
+
+    def c_copy(zi, xi, k):
+        return g_copy(at(zi, xi, c), k, ac_s.at[zi, xi, k], at(z, x, other))
+
+    def arrived(slot, k):
+        g_copy(slot, k, ac_s.at[0, 0, k], at(z, x, other)).wait_recv()
+
+    for k in range(PIECES):
+        for d in range(1, nh):
+            y_arrival(d, k).wait_recv()
+        total = feat[span(k), cols(h)].astype(F32)
+        for d in range(1, nh):
+            total = total + ybuf[lax.rem(h + d, nh), span(k)].astype(F32)
+        gat[me, span(k)] = total.astype(BF16)
+
+        @pl.when(z + 1 < nz)
+        def _(k=k):
+            right_copy(z, k).start()
+
+        @pl.when(z >= 1)
+        def _(k=k):
+            left_copy(z, k).start()
+
+        for d in range(1, nx):
+            x_copy(z, d, k).start()
+        c_copy(z, x, k).start()
 
     place_ref[...] = jnp.zeros_like(place_ref)
     idxb[me] = idx[me]
     chunk = min(256, rows_dev)
-    batch = gat.shape[1]
 
     def proc(slot):
         meta = idxb[slot]
@@ -169,25 +188,8 @@
 
     proc(me)
 
-    def z_body(d, carry):
-        zi = zof(d)
-        slot = at(zi, x, c)
-        arrived(slot)
-        for dx in range(1, nx):
-            x_copy(zi, dx).start()
-        c_copy(zi, x).start()
-        i_arrival(slot).wait_recv()
-        proc(slot)
-        return carry
-
-    lax.fori_loop(1, nz, z_body, 0)
-
-    core_copy(x).wait_recv()
-    for d in range(1, nx):
-        rx_arrival(d).wait_recv()
-
     def own_sum(k):
-        s = grad[k, x, c].astype(F32) + rcore[k, x].astype(F32)
+        s = grad[k, x, c] + rcore[k, x]
         for d in range(1, nx):
             s = s + rx[xof(d), k].astype(F32)
         return s
@@ -206,26 +208,64 @@
         rz_copy(d).start()
         return carry
 
-    lax.fori_loop(1, nz, rz_start, 0)
-
-    def x_body(k, carry):
-        zi = zof(k // (nx - 1))
-        xi = xof(1 + lax.rem(k, nx - 1))
-        slot = at(zi, xi, c)
-        arrived(slot)
-        c_copy(zi, xi).start()
+    def from_z(zi, open_end, onward):
+        slot = at(zi, x, c)
+        for k in range(PIECES):
+            arrived(slot, k)
+
+            @pl.when(open_end)
+            def _(k=k):
+                onward(zi, k).start()
+
+            for dx in range(1, nx):
+                x_copy(zi, dx, k).start()
+            c_copy(zi, x, k).start()
         i_arrival(slot).wait_recv()
         proc(slot)
-        return carry
-
-    if nx > 1:
-        lax.fori_loop(0, nz * (nx - 1), x_body, 0)
+
+    def from_x(zi):
+        for dx in range(1, nx):
+            slot = at(zi, xof(dx), c)
+            for k in range(PIECES):
+                arrived(slot, k)
+                c_copy(zi, xof(dx), k).start()
+            i_arrival(slot).wait_recv()
+            proc(slot)
+
+    def line_body(j, carry):
+        @pl.when(z - j >= 0)
+        def _():
+            from_z(z - j, z + 1 < nz, right_copy)
+
+        @pl.when(z + j < nz)
+        def _():
+            from_z(z + j, z >= 1, left_copy)
+
+        @pl.when(j == (nz + 1) // 2)
+        def _():
+            core_copy(x).wait_recv()
+            for d in range(1, nx):
+                rx_arrival(d).wait_recv()
+            lax.fori_loop(1, nz, rz_start, 0)
+
+        @pl.when(z - j + 1 >= 0)
+        def _():
+            from_x(z - j + 1)
+
+        @pl.when((j > 1) & (z + j - 1 < nz))
+        def _():
+            from_x(z + j - 1)
+
+        return carry
+
+    lax.fori_loop(1, nz + 1, line_body, 0)
 
     def c_body(k, carry):
         j = k // nz
         zi = zof(lax.rem(k, nz))
         slot = at(zi, xof(j), other)
-        arrived(slot)
+        for p in range(PIECES):
+            arrived(slot, p)
         i_arrival(slot).wait_recv()
         proc(slot)
         return carry
@@ -241,8 +281,9 @@
 
     lax.fori_loop(1, nz, rz_end, 0)
 
-    for d in range(1, nh):
-        y_copy(d).wait_send()
+    for p in range(PIECES):
+        for d in range(1, nh):
+            y_copy(d, p).wait_send()
     for d in range(1, nx + 1):
         core_copy(xof(d)).wait_send()
     for d in range(1, nx):
@@ -255,17 +296,26 @@
     lax.fori_loop(1, n, i_end, 0)
 
     def z_end(d, carry):
-        z_copy(d).wait_send()
         rz_copy(d).wait_send()
         return carry
 
     lax.fori_loop(1, nz, z_end, 0)
 
     def end_all(k, carry):
-        for dx in range(1, nx):
-            x_copy(k, dx).wait_send()
-        for xi in range(nx):
-            c_copy(k, xi).wait_send()
+        for p in range(PIECES):
+
+            @pl.when((k <= z) & (z + 1 < nz))
+            def _(p=p):
+                right_copy(k, p).wait_send()
+
+            @pl.when((k >= z) & (z >= 1))
+            def _(p=p):
+                left_copy(k, p).wait_send()
+
+            for dx in range(1, nx):
+                x_copy(k, dx, p).wait_send()
+            for xi in range(nx):
+                c_copy(k, xi, p).wait_send()
         return carry
 
     lax.fori_loop(0, nz, end_all, 0)
@@ -278,7 +328,6 @@
 ):
     slots = place.shape[0]
     list_len = evict_slots.shape[0]
-    keep = send_accum.shape[0] * send_accum.shape[1]
     step = 16
 
     def scatter(i, carry):
@@ -315,9 +364,51 @@
 
     lax.fori_loop(0, list_len // 8, evict, 0)
     groups = send_accum.shape[0]
-    cap = keep // groups
+    cap = send_accum.shape[2]
     for d in range(groups):
-        send_accum[d : d + 1, :] = jnp.max(sgrad[d * cap : (d + 1) * cap, :], axis=-1)[None, :]
+        send_accum[d] = jnp.max(sgrad[d * cap : (d + 1) * cap, :], axis=-1)[None, :]
+
+
+def hold_kernel(nh, rows, accum, held_rows, held_accum, rbuf, abuf, r_s, r_r, a_s, a_r):
+    h = lax.axis_index("hst")
+    cap = rbuf.shape[1]
+    barrier = pltpu.get_barrier_semaphore()
+    for d in range(1, nh):
+        pl.semaphore_signal(
+            barrier, inc=1, device_id={"hst": lax.rem(h + d, nh)}, device_id_type=MESH
+        )
+    pl.semaphore_wait(barrier, nh - 1)
+
+    def part(k):
+        return pl.ds(pl.multiple_of(k * cap, cap), cap)
+
+    def copies(d, slot):
+        k = lax.rem(h + d, nh)
+        return [
+            pltpu.make_async_remote_copy(
+                src_ref=src, dst_ref=dst.at[slot], send_sem=s.at[d], recv_sem=r.at[slot],
+                device_id={"hst": k}, device_id_type=MESH,
+            )
+            for src, dst, s, r in (
+                (rows.at[part(k)], rbuf, r_s, r_r),
+                (accum.at[k], abuf, a_s, a_r),
+            )
+        ]
+
+    for d in range(1, nh):
+        for copy in copies(d, h):
+            copy.start()
+    held_rows[h] = rows[part(h), :]
+    held_accum[h] = accum[h]
+    for d in range(1, nh):
+        k = lax.rem(h + d, nh)
+        for copy in copies(d, k):
+            copy.wait_recv()
+        held_rows[k] = rbuf[k]
+        held_accum[k] = abuf[k]
+    for d in range(1, nh):
+        for copy in copies(d, h):
+            copy.wait_send()
 
 
 def on_device(
@@ -343,7 +434,7 @@
     ).astype(BF16)
     grad = lax.dot_general(
         pooled, delta, (((0,), (0,)), ((), ())), preferred_element_type=F32
-    ).astype(BF16)
+    )
     grad = grad.reshape(nz, nx, 2, out_rows, hid)
 
     own_t = jnp.transpose(owners, (2, 0, 1))
@@ -370,13 +461,14 @@
             pltpu.VMEM((nh, batch, width), BF16),
             pltpu.VMEM((n, batch, width), BF16),
             pltpu.VMEM((n, 2 * tables, batch), F32),
-            pltpu.VMEM((nz, nx, out_rows, hid), BF16),
+            pltpu.VMEM((nz, nx, out_rows, hid), F32),
             pltpu.VMEM((nz, nx, out_rows, hid), BF16),
             pltpu.VMEM((nx, nz, out_rows, hid), BF16),
             pltpu.VMEM((nz, out_rows, hid), BF16),
             pltpu.VMEM((nz, out_rows, hid), BF16),
-            dma((nh,)), dma((nh,)), dma((n,)), dma((n,)),
-            dma((nz,)), dma((nz, nx)), dma((nz, nx)), dma((n,)),
+            dma((nh, PIECES)), dma((nh, PIECES)), dma((n,)), dma((n,)),
+            dma((nz, PIECES)), dma((nz, PIECES)), dma((nz, nx, PIECES)), dma((nz, nx, PIECES)),
+            dma((n, PIECES)),
             dma((nx,)), dma((nx,)), dma((nx,)), dma((nx,)), dma((nz,)), dma((nz,)),
         ],
         compiler_params=pltpu.CompilerParams(
@@ -400,7 +492,7 @@
             jax.ShapeDtypeStruct((slots, emb), F32),
             jax.ShapeDtypeStruct((slots // 128, 128), F32),
             jax.ShapeDtypeStruct((nh * cap + 8, emb), F32),
-            jax.ShapeDtypeStruct((nh, cap), F32),
+            jax.ShapeDtypeStruct((nh, 1, cap), F32),
         ),
         in_specs=[smem] * 3 + [vmem] * 3,
         out_specs=(vmem,) * 4,
@@ -410,17 +502,28 @@
         slot_map.reshape(slots), chosen, goal.astype(jnp.int32), place,
         cache_weight.reshape(slots, emb), cache_accum.reshape(slots // 128, 128),
     )
-    pad = -(-cap // emb)
-    both = jnp.concatenate(
-        [send_rows[: nh * cap].reshape(nh, cap, emb), send_accum.reshape(nh, pad, emb)], axis=1
-    )
-    both = lax.all_to_all(both, "hst", split_axis=0, concat_axis=0, tiled=True)
+    held_rows, held_accum = pl.pallas_call(
+        functools.partial(hold_kernel, nh),
+        out_shape=(
+            jax.ShapeDtypeStruct((nh, cap, emb), F32),
+            jax.ShapeDtypeStruct((nh, 1, cap), F32),
+        ),
+        in_specs=[vmem, vmem],
+        out_specs=(vmem, vmem),
+        scratch_shapes=[
+            pltpu.VMEM((nh, cap, emb), F32),
+            pltpu.VMEM((nh, 1, cap), F32),
+            dma((nh,)), dma((nh,)), dma((nh,)), dma((nh,)),
+        ],
+        compiler_params=pltpu.CompilerParams(collective_id=1, has_side_effects=True),
+        name="hold",
+    )(send_rows, send_accum)
     return (
         grad_up,
         new_weight[None, None],
         new_accum.reshape(1, 1, slots),
-        both[:, :cap][None, None],
-        both[:, cap:].reshape(1, 1, nh, cap),
+        held_rows[None, None],
+        held_accum.reshape(1, 1, nh, cap),
     )
 
 

time: 98.6 us -> 90 us (0.913)
  the two profiles are of different devices: /device:TPU:10 before, /device:TPU:0 now
where the time goes in v2:
time: 90 us; the launch traced here: 89.7 us
  Pallas kernels  71.8 us (80%)
  matrix products  9.38 us (10%)
  local copies, waits for them, and re-layouts  5.12 us (6%)
  other arithmetic  1.94 us (2%)
  between operations  1.46 us (2%)
    pallas_call x1, Pallas kernels, on_device(): pl.pallas_call(functools.partial(exchange_kernel, nz, nx, nh, tables, row...  57.1 us
    pallas_call x1, Pallas kernels, on_device(): pl.pallas_call(update_kernel, out_shape=(jax.ShapeDtypeStruct((slots, emb...  8.71 us
    pallas_call x1, Pallas kernels, on_device(): pl.pallas_call(functools.partial(hold_kernel, nh), out_shape=(jax.ShapeDt...  5.99 us
    unnamed x19, local copies, waits for them, and re-layouts  5.12 us
    dot_general x1, matrix products, on_device(): preact = jnp.dot(pooled, w_up, preferred_element_type=F32)  4.03 us
    dot_general x1, matrix products, on_device(): lax.dot_general(pooled, delta, (((0,), (0,)), ((), ())), preferred_elemen...  3.26 us
    dot_general x1, matrix products, on_device(): lax.dot_general(delta, w_up, (((1,), (1,)), ((), ())), preferred_element_...  2.09 us

profile of v2, /device:TPU:0, one launch (start us, length us, event | category | flops | bytes accessed | tf_op | source)
XLA Modules:
  0.0 89.7 jit_solution(8206206735214477058)
XLA Ops:
  0.6 0.0 copy-start
  0.6 1.6 %copy-done = bf16[512,2048]{1,0:T(8,128)(2,1)S(1)} copy-done((bf16[512,2048]{1,0:T(8,128)(2,1)S(1)}, bf16[512,2048]{1,0:T(8,128)(2,1)}, u32[]{:S(2)}) %copy-start) | copy-done | bytes 2097176
  2.2 4.0 %multiply_convert_fusion = bf16[512,2048]{1,0:T(8,128)(2,1)S(1)} fusion(bf16[512,2048]{1,0:T(8,128)(2,1)} %param.15, bf16[512,512]{1,0:T(8,128)(2,1)} %param.13, bf16[512,2048]{1,0:T(8,128)(2,1)S(1)} %copy-done), kind=kOutput, calls=%fused_computation | convolution fusion | flops 1084227584 | bytes 6815744 | tf_op jit(solution)/shard_map/dot_general | solution.py:429
  6.3 0.0 copy-start.1
  6.3 2.1 %convolution_convert_fusion.feat = bf16[512,512]{1,0:T(8,128)(2,1)} fusion(bf16[512,2048]{1,0:T(8,128)(2,1)S(1)} %multiply_convert_fusion, bf16[512,2048]{1,0:T(8,128)(2,1)S(1)} %copy-done), kind=kOutput, calls=%fused_computation.1 | convolution fusion | flops 1074003968 | bytes 4718592 | tf_op jit(solution)/shard_map/dot_general | solution.py:432
  8.4 0.0 copy-done.1
  8.4 0.0 copy-start.3
  8.4 0.0 copy-start.7
  8.4 0.0 copy-start.5
  8.4 0.0 copy-start.4
  8.4 3.3 %fusion.3 = f32[2048,512]{0,1:T(8,128)} fusion(bf16[512,2048]{1,0:T(8,128)(2,1)S(1)} %multiply_convert_fusion, bf16[512,512]{1,0:T(8,128)(2,1)S(1)} %copy-done.1), kind=kOutput, calls=%fused_computation.17 | convolution fusion | flops 1073741824 | bytes 6815744 | tf_op jit(solution)/shard_map/dot_general | solution.py:435
  11.7 0.0 copy-done.3
  11.7 0.0 copy-done.7
  11.7 0.0 copy-done.5
  11.7 0.0 copy-done.4
  11.7 0.4 select_reduce_fusion.1
  12.2 0.7 pad_maximum_fusion.idx
  12.9 0.0 copy-start.6
  12.9 57.1 %exchange.1 = (f32[32,2048]{1,0:T(8,128)}, f32[2048,128]{1,0:T(8,128)}) custom-call(bf16[512,512]{1,0:T(8,128)(2,1)} %convolution_convert_fusion.feat, f32[4,2,2,32,2048]{4,3,2,1,0:T(8,128)} %bitcast.26, f32[16,4,512]{2,1,0:T(4,128)} %pad_maximum_fusion.idx), custom_call_target="tpu_custom_call" | custom-call | tf_op jit(solution)/shard_map/exchange/pallas_call | solution.py:452
  70.0 0.0 copy-start.2
  70.7 0.0 copy-done.6
  70.7 0.2 convert_reduce_fusion
  70.9 0.6 add_select_fusion.goal
  71.5 8.7 %update.1 = (f32[2048,128]{1,0:T(8,128)}, f32[16,128]{1,0:T(8,128)}, f32[264,128]{1,0:T(8,128)}, f32[2,1,128]{2,1,0:T(1,128)}) custom-call(s32[2048]{0:T(1024)} %bitcast.32, s32[256]{0:T(256)} %bitcast.34, s32[256]{0:T(256)} %add_select_fusion.goal, f32[2048,128]{1,0:T(8,128)} %get-tuple-element.14.place, f32[2048,128]{1,0:T(8,128)} %bitcast.27, ...), custom_call_target="tpu_custom_call" | custom-call | tf_op jit(solution)/shard_map/update/pallas_call | solution.py:489
  80.2 6.0 %hold.1 = (f32[2,128,128]{2,1,0:T(8,128)}, f32[2,1,128]{2,1,0:T(1,128)}) custom-call(f32[264,128]{1,0:T(8,128)} %get-tuple-element.17.rows, f32[2,1,128]{2,1,0:T(1,128)} %get-tuple-element.18.accum), custom_call_target="tpu_custom_call" | custom-call | tf_op jit(solution)/shard_map/hold/pallas_call | solution.py:505
  86.2 0.0 copy-done.2
  86.2 0.7 copy.25
  86.9 1.6 %copy.26 = f32[1,1,2,128,128]{4,3,2,1,0:T(8,128)} copy(f32[1,1,2,128,128]{4,3,2,1,0:T(8,128)} %bitcast.28) | data formatting | bytes 262144
  88.5 1.2 %copy.27 = f32[1,1,2,128]{3,2,1,0:T(2,128)} copy(f32[1,1,2,128]{3,2,1,0:T(2,128)} %bitcast.35) | data formatting | bytes 2048
  (5 shorter events, 0.1 us)
Async XLA Ops:
  0.6 1.6 %copy-start = (bf16[512,2048]{1,0:T(8,128)(2,1)S(1)}, bf16[512,2048]{1,0:T(8,128)(2,1)}, u32[]{:S(2)}) copy-start(bf16[512,2048]{1,0:T(8,128)(2,1)} %param.14) | copy-start | bytes 6291460
  6.3 2.1 %copy-start.1 = (bf16[512,512]{1,0:T(8,128)(2,1)S(1)}, bf16[512,512]{1,0:T(8,128)(2,1)}, u32[]{:S(2)}) copy-start(bf16[512,512]{1,0:T(8,128)(2,1)} %param.13) | copy-start | bytes 1572868
  8.4 3.3 %copy-start.3 = (s32[2,512,8]{1,2,0:T(8,128)S(1)}, s32[2,512,8]{1,2,0:T(8,128)}, u32[]{:S(2)}) copy-start(s32[2,512,8]{1,2,0:T(8,128)} %param.17) | copy-start | bytes 98308
  8.4 3.3 %copy-start.7 = (s32[2,512]{1,0:T(2,128)S(1)}, s32[2,512]{1,0:T(2,128)}, u32[]{:S(2)}) copy-start(s32[2,512]{1,0:T(2,128)} %param.19) | copy-start | bytes 12292
  8.4 3.3 %copy-start.5 = (bf16[2,512,8]{1,2,0:T(8,128)(2,1)S(1)}, bf16[2,512,8]{1,2,0:T(8,128)(2,1)}, u32[]{:S(2)}) copy-start(bf16[2,512,8]{1,2,0:T(8,128)(2,1)} %param.18) | copy-start | bytes 49156
  8.4 3.3 %copy-start.4 = (s32[2,512,8]{1,2,0:T(8,128)S(1)}, s32[2,512,8]{1,2,0:T(8,128)}, u32[]{:S(2)}) copy-start(s32[2,512,8]{1,2,0:T(8,128)} %param.16) | copy-start | bytes 98308
  12.9 57.8 %copy-start.6 = (s32[1,1,256]{2,1,0:T(1,128)S(1)}, s32[1,1,256]{2,1,0:T(1,128)}, u32[]{:S(2)}) copy-start(s32[1,1,256]{2,1,0:T(1,128)} %param.24) | copy-start | bytes 3076
  70.0 16.2 %copy-start.2 = (f32[32,2048]{1,0:T(8,128)S(1)}, f32[32,2048]{1,0:T(8,128)}, u32[]{:S(2)}) copy-start(f32[32,2048]{1,0:T(8,128)} %get-tuple-element.28) | copy-start | bytes 786436

commit v3 on v2

--- a/solution.py
+++ b/solution.py
@@ -10,7 +10,7 @@
 LEARN_RATE = 0.05
 EPSILON = 1e-08
 MESH = pl.DeviceIdType.MESH
-PIECES = 2
+PIECES = 4
 F32 = jnp.float32
 BF16 = jnp.bfloat16
 

time: 90 us -> 90.2 us (level)
  no operation moved by 1% of the time
where the time goes in v3:
time: 90.2 us; the launch traced here: 89.9 us
  Pallas kernels  72 us (80%)
  matrix products  9.38 us (10%)
  local copies, waits for them, and re-layouts  5.12 us (6%)
  other arithmetic  1.94 us (2%)
  between operations  1.46 us (2%)
    pallas_call x1, Pallas kernels, on_device(): pl.pallas_call(functools.partial(exchange_kernel, nz, nx, nh, tables, row...  57.3 us
    pallas_call x1, Pallas kernels, on_device(): pl.pallas_call(update_kernel, out_shape=(jax.ShapeDtypeStruct((slots, emb...  8.71 us
    pallas_call x1, Pallas kernels, on_device(): pl.pallas_call(functools.partial(hold_kernel, nh), out_shape=(jax.ShapeDt...  5.99 us
    unnamed x19, local copies, waits for them, and re-layouts  5.12 us
    dot_general x1, matrix products, on_device(): preact = jnp.dot(pooled, w_up, preferred_element_type=F32)  4.03 us
    dot_general x1, matrix products, on_device(): lax.dot_general(pooled, delta, (((0,), (0,)), ((), ())), preferred_elemen...  3.26 us
    dot_general x1, matrix products, on_device(): lax.dot_general(delta, w_up, (((1,), (1,)), ((), ())), preferred_element_...  2.09 us

profile of v3, /device:TPU:0, one launch (start us, length us, event | category | flops | bytes accessed | tf_op | source)
XLA Modules:
  0.0 89.9 jit_solution(1860863859233971718)
XLA Ops:
  0.6 0.0 copy-start
  0.6 1.6 %copy-done = bf16[512,2048]{1,0:T(8,128)(2,1)S(1)} copy-done((bf16[512,2048]{1,0:T(8,128)(2,1)S(1)}, bf16[512,2048]{1,0:T(8,128)(2,1)}, u32[]{:S(2)}) %copy-start) | copy-done | bytes 2097176
  2.2 4.0 %multiply_convert_fusion = bf16[512,2048]{1,0:T(8,128)(2,1)S(1)} fusion(bf16[512,2048]{1,0:T(8,128)(2,1)} %param.15, bf16[512,512]{1,0:T(8,128)(2,1)} %param.13, bf16[512,2048]{1,0:T(8,128)(2,1)S(1)} %copy-done), kind=kOutput, calls=%fused_computation | convolution fusion | flops 1084227584 | bytes 6815744 | tf_op jit(solution)/shard_map/dot_general | solution.py:429
  6.3 0.0 copy-start.1
  6.3 2.1 %convolution_convert_fusion.feat = bf16[512,512]{1,0:T(8,128)(2,1)} fusion(bf16[512,2048]{1,0:T(8,128)(2,1)S(1)} %multiply_convert_fusion, bf16[512,2048]{1,0:T(8,128)(2,1)S(1)} %copy-done), kind=kOutput, calls=%fused_computation.1 | convolution fusion | flops 1074003968 | bytes 4718592 | tf_op jit(solution)/shard_map/dot_general | solution.py:432
  8.4 0.0 copy-done.1
  8.4 0.0 copy-start.3
  8.4 0.0 copy-start.7
  8.4 0.0 copy-start.5
  8.4 0.0 copy-start.4
  8.4 3.3 %fusion.3 = f32[2048,512]{0,1:T(8,128)} fusion(bf16[512,2048]{1,0:T(8,128)(2,1)S(1)} %multiply_convert_fusion, bf16[512,512]{1,0:T(8,128)(2,1)S(1)} %copy-done.1), kind=kOutput, calls=%fused_computation.17 | convolution fusion | flops 1073741824 | bytes 6815744 | tf_op jit(solution)/shard_map/dot_general | solution.py:435
  11.7 0.0 copy-done.3
  11.7 0.0 copy-done.7
  11.7 0.0 copy-done.5
  11.7 0.0 copy-done.4
  11.7 0.4 select_reduce_fusion.1
  12.2 0.7 pad_maximum_fusion.idx
  12.9 0.0 copy-start.6
  12.9 57.3 %exchange.1 = (f32[32,2048]{1,0:T(8,128)}, f32[2048,128]{1,0:T(8,128)}) custom-call(bf16[512,512]{1,0:T(8,128)(2,1)} %convolution_convert_fusion.feat, f32[4,2,2,32,2048]{4,3,2,1,0:T(8,128)} %bitcast.26, f32[16,4,512]{2,1,0:T(4,128)} %pad_maximum_fusion.idx), custom_call_target="tpu_custom_call" | custom-call | tf_op jit(solution)/shard_map/exchange/pallas_call | solution.py:452
  70.2 0.0 copy-start.2
  70.9 0.0 copy-done.6
  70.9 0.2 convert_reduce_fusion
  71.1 0.6 add_select_fusion.goal
  71.7 8.7 %update.1 = (f32[2048,128]{1,0:T(8,128)}, f32[16,128]{1,0:T(8,128)}, f32[264,128]{1,0:T(8,128)}, f32[2,1,128]{2,1,0:T(1,128)}) custom-call(s32[2048]{0:T(1024)} %bitcast.32, s32[256]{0:T(256)} %bitcast.34, s32[256]{0:T(256)} %add_select_fusion.goal, f32[2048,128]{1,0:T(8,128)} %get-tuple-element.14.place, f32[2048,128]{1,0:T(8,128)} %bitcast.27, ...), custom_call_target="tpu_custom_call" | custom-call | tf_op jit(solution)/shard_map/update/pallas_call | solution.py:489
  80.4 6.0 %hold.1 = (f32[2,128,128]{2,1,0:T(8,128)}, f32[2,1,128]{2,1,0:T(1,128)}) custom-call(f32[264,128]{1,0:T(8,128)} %get-tuple-element.17.rows, f32[2,1,128]{2,1,0:T(1,128)} %get-tuple-element.18.accum), custom_call_target="tpu_custom_call" | custom-call | tf_op jit(solution)/shard_map/hold/pallas_call | solution.py:505
  86.4 0.0 copy-done.2
  86.4 0.7 copy.25
  87.1 1.6 %copy.26 = f32[1,1,2,128,128]{4,3,2,1,0:T(8,128)} copy(f32[1,1,2,128,128]{4,3,2,1,0:T(8,128)} %bitcast.28) | data formatting | bytes 262144
  88.7 1.2 %copy.27 = f32[1,1,2,128]{3,2,1,0:T(2,128)} copy(f32[1,1,2,128]{3,2,1,0:T(2,128)} %bitcast.35) | data formatting | bytes 2048
  (5 shorter events, 0.1 us)
Async XLA Ops:
  0.6 1.6 %copy-start = (bf16[512,2048]{1,0:T(8,128)(2,1)S(1)}, bf16[512,2048]{1,0:T(8,128)(2,1)}, u32[]{:S(2)}) copy-start(bf16[512,2048]{1,0:T(8,128)(2,1)} %param.14) | copy-start | bytes 6291460
  6.3 2.1 %copy-start.1 = (bf16[512,512]{1,0:T(8,128)(2,1)S(1)}, bf16[512,512]{1,0:T(8,128)(2,1)}, u32[]{:S(2)}) copy-start(bf16[512,512]{1,0:T(8,128)(2,1)} %param.13) | copy-start | bytes 1572868
  8.4 3.3 %copy-start.3 = (s32[2,512,8]{1,2,0:T(8,128)S(1)}, s32[2,512,8]{1,2,0:T(8,128)}, u32[]{:S(2)}) copy-start(s32[2,512,8]{1,2,0:T(8,128)} %param.17) | copy-start | bytes 98308
  8.4 3.3 %copy-start.7 = (s32[2,512]{1,0:T(2,128)S(1)}, s32[2,512]{1,0:T(2,128)}, u32[]{:S(2)}) copy-start(s32[2,512]{1,0:T(2,128)} %param.19) | copy-start | bytes 12292
  8.4 3.3 %copy-start.5 = (bf16[2,512,8]{1,2,0:T(8,128)(2,1)S(1)}, bf16[2,512,8]{1,2,0:T(8,128)(2,1)}, u32[]{:S(2)}) copy-start(bf16[2,512,8]{1,2,0:T(8,128)(2,1)} %param.18) | copy-start | bytes 49156
  8.4 3.3 %copy-start.4 = (s32[2,512,8]{1,2,0:T(8,128)S(1)}, s32[2,512,8]{1,2,0:T(8,128)}, u32[]{:S(2)}) copy-start(s32[2,512,8]{1,2,0:T(8,128)} %param.16) | copy-start | bytes 98308
  12.9 58.0 %copy-start.6 = (s32[1,1,256]{2,1,0:T(1,128)S(1)}, s32[1,1,256]{2,1,0:T(1,128)}, u32[]{:S(2)}) copy-start(s32[1,1,256]{2,1,0:T(1,128)} %param.24) | copy-start | bytes 3076
  70.2 16.2 %copy-start.2 = (f32[32,2048]{1,0:T(8,128)S(1)}, f32[32,2048]{1,0:T(8,128)}, u32[]{:S(2)}) copy-start(f32[32,2048]{1,0:T(8,128)} %get-tuple-element.28) | copy-start | bytes 786436
